TPU v7x, 256 devices: a whole 4x4x8 slice. The times are simulated.
256 devices in a mesh: side: 2 (over x_hi), row: 32 (over y, z), col: 4 (over x_lo, core).
Axes of the slice: x: 4 (x_hi: 2, x_lo: 2; x = x_hi * 2 + x_lo), y: 4, z: 8, core: 2. Of those that a mesh axis runs over, the one named last changes fastest.
Arguments:
- old_vectors: bfloat16 [2, 32768, 16384], P('side', 'row', 'col'), may hold values from -6 to 6
- reflectors: bfloat16 [2, 2, 32768, 512], P('side', None, 'row', 'col'), may hold values from -0.0625 to 0.0625
- triangles: float32 [2, 2, 512, 512], P('side'), may hold values from -0.25 to 0.25
- pole_sq: float32 [32768], replicated, may hold values from 1 to 65536, as said below
- coupling: float32 [32768], replicated, may hold values from -1 to 1
- deflated: int32 [32768], replicated, may hold values 0 or 1
- pole_order: int32 [32768], replicated, may hold values from 0 to 32767, each once
- anchors: int32 [1024], replicated, may hold values from 0 to 32766, as said below
- root_fraction: float32 [1024], replicated, may hold values from 0.2 to 0.8
Outputs:
- vectors: bfloat16 [2, 1024, 32768], P('side', 'col', 'row')
Inputs may be any that keep to these rules, and one draw needn't show every extreme that they name: `pole_sq`: strictly increasing; successive entries differ by 0.5 or more. `anchors`: distinct entries.
All inputs are finite; a program needn't handle non-finite values.
Results may differ from a plain program's by a relative error of at most 0.014.
Values may be sent and summed in bfloat16 or wider, within the bound.
A program may use at most 128 MiB of HBM per device.

v0:
```python
import jax
import jax.numpy as jnp
from jax import lax
from jax.sharding import PartitionSpec as P


def secular_columns(col_sq, col_coupling, col_live, weight, anchor_sq, pole_gap, root_fraction):
    denom = col_sq[:, None] - anchor_sq[None, :] - root_fraction[None, :] * pole_gap[None, :]
    return (col_live * col_coupling * weight)[:, None] / denom


def per_device(
    old_vectors,
    reflectors,
    triangles,
    pole_sq,
    coupling,
    deflated,
    pole_order,
    anchors,
    root_fraction,
):
    side_index = lax.axis_index("side")
    row_index = lax.axis_index("row")
    col_index = lax.axis_index("col")
    half_rows = lax.axis_size("row") // 2
    col_count = lax.axis_size("col")
    old_block = old_vectors[0]
    col_width = old_block.shape[1]
    order_size = pole_sq.shape[0]
    triplets = anchors.shape[0]
    local_triplets = triplets // col_count
    first_column = row_index // half_rows * (order_size // 2) + col_index * col_width
    columns = first_column + jnp.arange(col_width, dtype=jnp.int32)
    position = (
        jnp.zeros((order_size,), jnp.int32)
        .at[pole_order]
        .set(jnp.arange(order_size, dtype=jnp.int32))
    )
    sorted_pos = lax.dynamic_slice_in_dim(position, first_column, col_width)
    col_sq = pole_sq[sorted_pos]
    col_coupling = coupling[sorted_pos]
    col_live = (1 - deflated[sorted_pos]).astype(jnp.float32)
    weight = jnp.where(side_index == 0, jnp.ones_like(col_sq), jnp.sqrt(col_sq))
    anchor_sq = pole_sq[anchors]
    pole_gap = pole_sq[anchors + 1] - anchor_sq
    dead_triplet = deflated[anchors] == 1
    target = pole_order[anchors]
    secular = secular_columns(
        col_sq, col_coupling, col_live, weight, anchor_sq, pole_gap, root_fraction
    )
    onehot = (columns[:, None] == target[None, :]).astype(jnp.float32)
    mixing = jnp.where(dead_triplet[None, :], onehot, secular).astype(jnp.bfloat16)
    share_size = col_width // half_rows
    slice_part = lax.dynamic_slice_in_dim(
        secular, row_index % half_rows * share_size, share_size, 0
    )
    squares = lax.psum(jnp.sum(slice_part * slice_part, axis=0), ("row", "col"))
    col_scale = jnp.where(dead_triplet, jnp.ones_like(squares), 1.0 / jnp.sqrt(squares + 1e-06))
    merged = lax.psum_scatter(
        jnp.einsum("ck,rc->kr", mixing, old_block, preferred_element_type=jnp.float32).astype(
            jnp.bfloat16
        ),
        "col",
        scatter_dimension=0,
        tiled=True,
    ).astype(jnp.float32)
    my_scale = lax.dynamic_slice_in_dim(col_scale, col_index * local_triplets, local_triplets)
    vectors = merged * my_scale[:, None]
    panel_local = reflectors[0]
    panels = panel_local.shape[0]
    upper_tri = jnp.triu(triangles[0])
    highest = lax.Precision.HIGHEST
    for panel_index in reversed(range(panels)):
        panel_rows = panel_local[panel_index]
        current = vectors
        current_low = current.astype(jnp.bfloat16)
        projected = jnp.dot(
            current_low,
            lax.all_gather(panel_rows, "col", axis=1, tiled=True),
            preferred_element_type=jnp.float32,
        )
        projected = lax.psum(projected.astype(jnp.bfloat16), "row").astype(jnp.float32)
        coefficients = jnp.dot(projected, upper_tri[panel_index].T, precision=highest).astype(
            jnp.bfloat16
        )
        vectors = current - jnp.dot(
            coefficients,
            lax.all_gather(panel_rows, "col", axis=1, tiled=True).T,
            preferred_element_type=jnp.float32,
        )
    return vectors.astype(jnp.bfloat16)[None]


def solution(mesh):
    in_specs = (
        P("side", "row", "col"),
        P("side", None, "row", "col"),
        P("side", None, None, None),
        P(),
        P(),
        P(),
        P(),
        P(),
        P(),
    )
    out_specs = P("side", "col", "row")
    return jax.shard_map(
        per_device, mesh=mesh, in_specs=in_specs, out_specs=out_specs, check_vma=False
    )
```

profile of v0, /device:TPU:2, one launch (start us, length us, event | category | flops | bytes accessed | tf_op | source)
XLA Modules:
  0.0 883.1 jit_solution(16158088718118967877)
XLA Ops:
  6.5 0.0 copy-start
  6.5 0.0 all-gather.5.cloned.1.call-start
  6.5 1.9 fusion.23
  8.4 0.0 all-gather.5.cloned.1.call-update
  8.4 0.0 reduce-scatter.2.cloned.1.call-start
  8.5 0.9 compare_select_fusion
  9.5 120.1 %scatter_custom_fusion = s32[32768]{0:T(1024)S(1)} fusion(s32[32768]{0:T(1024)S(1)} %compare_select_fusion, s32[32768]{0:T(1024)S(1)} %iota.24, s32[]{:T(128)} %constant.23.clone.1), kind=kCustom, calls=%fused_computation.38 | custom fusion | bytes 131076 | tf_op jit(solution)/shard_map/scatter | solution.py:38
  129.6 0.0 copy-start.4
  129.6 0.0 copy-start.1
  129.6 19.5 %gather_fusion.2 = s32[4096]{0:T(1024)S(1)} fusion(s32[32768]{0:T(1024)} %param.14, s32[4096]{0:T(1024)S(1)} %fusion.20), kind=kCustom, calls=%fused_computation.2 | custom fusion | bytes 49152 | tf_op jit(solution)/shard_map/gather | solution.py:43
  149.2 0.0 copy-done
  149.2 0.0 copy-start.3
  149.2 0.0 copy-start.2
  149.2 23.0 %gather_fusion.4 = f32[4096]{0:T(1024)S(1)} fusion(f32[32768]{0:T(1024)S(1)} %copy-done, s32[4096]{0:T(1024)S(1)} %fusion.20), kind=kCustom, calls=%fused_computation.4 | custom fusion | bytes 49152 | tf_op jit(solution)/shard_map/gather | solution.py:41
  172.2 0.0 copy-done.4
  172.3 0.0 copy-start.5
  172.3 6.2 gather_fusion.5
  178.4 0.0 copy-done.1
  178.4 6.2 gather_fusion
  184.6 0.0 copy-done.3
  184.6 6.2 gather_fusion.1
  190.8 0.0 copy-done.2
  190.8 23.0 %gather_fusion.3 = f32[4096]{0:T(1024)S(1)} fusion(f32[32768]{0:T(1024)S(1)} %copy-done.2, s32[4096]{0:T(1024)S(1)} %fusion.20), kind=kCustom, calls=%fused_computation.3 | custom fusion | bytes 49152 | tf_op jit(solution)/shard_map/gather | solution.py:42
  213.8 6.2 gather_fusion.6
  220.0 0.0 copy-done.5
  220.0 6.5 subtract_divide_fusion
  226.5 1.3 multiply_reduce_fusion
  227.8 278.5 %psum.21 = f32[1024]{0:T(1024)S(1)} all-reduce(f32[1024]{0:T(1024)S(1)} %multiply_reduce_fusion), channel_id=1, replica_groups=mesh['side'=2,'row'=32,'col'=4] {'row','col'}, use_global_device_ids=true, to_apply=%region_3.4 | all-reduce | flops 1024 | bytes 8192 | tf_op jit(solution)/shard_map/psum | solution.py:58
  506.3 15.3 %fusion.5 = bf16[1024,1024]{1,0:T(8,128)(2,1)} fusion(bf16[1,1024,4096]{2,1,0:T(8,128)(2,1)} %param.9, s32[1024]{0:T(1024)S(1)} %gather_fusion.1, s32[4096]{0:T(1024)S(1)} %iota_add_fusion, pred[1024]{0:T(1024)(128)(4,1)S(1)} %get-tuple-element.6, f32[1024]{0:T(1024)S(1)} %subtract_multiply_fusion, f32[1024]{0:T(1024)S(1)} %gather_fusion.5, ...), kind=kOutput, calls=%fused_computation.16 | convolution fusion | flops 8620343296 | bytes 10548224 | tf_op jit(solution)/shard_map/ck,rc->kr/dot_general | solution.py:61
  521.7 0.0 reduce-scatter.2.cloned.1.call-update
  521.7 0.0 all-reduce.3.cloned.1.call-start
  521.8 0.1 dynamic_slice.11
  521.8 0.0 all-gather.5.cloned.1.call-done
  521.8 28.4 %reduce-scatter.2.cloned.1.call-done = bf16[256,1024]{1,0:T(8,128)(2,1)} async-done(((bf16[1024,1024]{1,0:T(8,128)(2,1)}), bf16[256,1024]{1,0:T(8,128)(2,1)}) %reduce-scatter.2.cloned.1.call-update) | async-done | bytes 524304 | tf_op jit(solution)/shard_map/reduce_scatter | solution.py:60
  550.3 2.6 convolution_convert_fusion.3
  552.9 0.0 all-reduce.3.cloned.1.call-update
  552.9 0.0 all-gather.7.cloned.1.call-start
  552.9 0.5 all-gather.7.cloned.1.call-update
  553.5 0.3 all-reduce.5.cloned.1.call-start
  553.7 0.2 iota_compare_fusion
  554.0 2.0 bitcast_select_fusion
  555.9 145.1 %all-reduce.3.cloned.1.call-done = bf16[256,512]{1,0:T(8,128)(2,1)} async-done(((bf16[256,512]{1,0:T(8,128)(2,1)}), bf16[256,512]{1,0:T(8,128)(2,1)}) %all-reduce.3.cloned.1.call-update) | async-done | bytes 262160 | tf_op jit(solution)/shard_map/psum | solution.py:83
  701.0 1.6 convolution_convert_fusion.2
  702.6 1.8 convolution_subtract_fusion.1
  704.5 18.7 %all-gather.7.cloned.1.call-done = bf16[1,1,1024,512]{3,2,1,0:T(8,128)(2,1)} async-done(((bf16[1,1,1024,128]{3,2,1,0:T(8,128)(2,1)}), bf16[1,1,1024,512]{3,2,1,0:T(8,128)(2,1)}) %all-gather.7.cloned.1.call-update) | async-done | bytes 1048592 | tf_op jit(solution)/shard_map/all_gather | solution.py:80
  723.1 2.4 convolution_convert_fusion.1
  725.5 0.0 all-reduce.5.cloned.1.call-update
  725.5 146.9 %all-reduce.5.cloned.1.call-done = bf16[256,512]{1,0:T(8,128)(2,1)} async-done(((bf16[256,512]{1,0:T(8,128)(2,1)}), bf16[256,512]{1,0:T(8,128)(2,1)}) %all-reduce.5.cloned.1.call-update) | async-done | bytes 262160 | tf_op jit(solution)/shard_map/psum | solution.py:83
  872.4 1.6 convolution_convert_fusion
  874.1 2.5 fusion.9
  (8 shorter events, 0.1 us)
Async XLA Ops:
  6.5 142.6 %copy-start = (f32[32768]{0:T(1024)S(1)}, f32[32768]{0:T(1024)}, u32[]{:S(2)}) copy-start(f32[32768]{0:T(1024)} %param.12) | copy-start | bytes 393220
  6.5 515.3 %all-gather.5.cloned.1.call-start = ((), (), s32[]{:S(2)}) async-start(), calls=%async_computation.4 | async-start | bytes 1310720 | tf_op jit(solution)/shard_map/all_gather | solution.py:80
  8.4 541.8 %reduce-scatter.2.cloned.1.call-start = ((), (), s32[]{:S(2)}) async-start(), calls=%async_computation.1 | async-start | bytes 2621440 | tf_op jit(solution)/shard_map/reduce_scatter | solution.py:60
  129.6 42.6 %copy-start.4 = (s32[1024]{0:T(1024)S(1)}, s32[1024]{0:T(1024)}, u32[]{:S(2)}) copy-start(s32[1024]{0:T(1024)} %param.16) | copy-start | bytes 12292
  129.6 48.8 %copy-start.1 = (s32[32768]{0:T(1024)S(1)}, s32[32768]{0:T(1024)}, u32[]{:S(2)}) copy-start(s32[32768]{0:T(1024)} %param.14) | copy-start | bytes 393220
  149.2 35.4 %copy-start.3 = (s32[32768]{0:T(1024)S(1)}, s32[32768]{0:T(1024)}, u32[]{:S(2)}) copy-start(s32[32768]{0:T(1024)} %param.15) | copy-start | bytes 393220
  149.2 41.6 %copy-start.2 = (f32[32768]{0:T(1024)S(1)}, f32[32768]{0:T(1024)}, u32[]{:S(2)}) copy-start(f32[32768]{0:T(1024)} %param.13) | copy-start | bytes 393220
  172.3 47.7 %copy-start.5 = (f32[1024]{0:T(1024)S(1)}, f32[1024]{0:T(1024)}, u32[]{:S(2)}) copy-start(f32[1024]{0:T(1024)} %param.17) | copy-start | bytes 12292
  521.7 179.3 %all-reduce.3.cloned.1.call-start = ((), (), s32[]{:S(2)}) async-start(), calls=%async_computation.2 | async-start | bytes 524288 | tf_op jit(solution)/shard_map/psum | solution.py:83
  552.9 170.3 %all-gather.7.cloned.1.call-start = ((), (), s32[]{:S(2)}) async-start(), calls=%async_computation.5 | async-start | bytes 1310720 | tf_op jit(solution)/shard_map/all_gather | solution.py:80
  553.5 319.0 %all-reduce.5.cloned.1.call-start = ((), (), s32[]{:S(2)}) async-start(), calls=%async_computation.3 | async-start | bytes 524288 | tf_op jit(solution)/shard_map/psum | solution.py:83
Sparse Core Ops, SparseCore 0:
  9.2 26.2 all-gather.4
  521.8 28.4 reduce-scatter.1
  554.1 146.8 all-reduce.2
  702.8 20.2 all-gather.6
  726.8 145.5 all-reduce.4
where the time goes:
time: 884 us; the launch traced here: 883 us
  waiting for transfers between devices  340 us (38%)
  blocking collectives  278 us (31%)
  local copies, waits for them, and re-layouts  212 us (24%)
  matrix products  27.8 us (3%)
  between operations  13.4 us (2%)
  other arithmetic  10.9 us (1%)
    psum x2, waiting for transfers between devices, per_device(): lax.psum(projected.astype(jnp.bfloat16), 'row').astype(jnp.float32)  292 us
    psum x1, blocking collectives, per_device(): squares = lax.psum(jnp.sum(slice_part * slice_part, axis=0), ('row', 'col'))  278 us
    scatter x1, local copies, waits for them, and re-layouts, per_device(): position = jnp.zeros((order_size,), jnp.int32).at[pole_order].set(jnp.ara...  120 us
    reduce_scatter x1, waiting for transfers between devices, per_device(): lax.psum_scatter(jnp.einsum('ck,rc->kr', mixing, old_block, preferred_ele...  28.4 us
    gather x1, local copies, waits for them, and re-layouts, per_device(): col_sq = pole_sq[sorted_pos]  23 us
    gather x1, local copies, waits for them, and re-layouts, per_device(): col_coupling = coupling[sorted_pos]  23 us
    gather x1, local copies, waits for them, and re-layouts, per_device(): col_live = (1 - deflated[sorted_pos]).astype(jnp.float32)  19.5 us
    all_gather x2, waiting for transfers between devices, per_device(): lax.all_gather(panel_rows, 'col', axis=1, tiled=True)  18.7 us
  transfers between devices with their start and end apart: 5, of which 4 were waited for; matrix products, arithmetic and copies ran while one was open for 27% of the time, Pallas kernels for 0%

commit v1 on v0

--- a/solution.py
+++ b/solution.py
@@ -80,7 +80,9 @@
             lax.all_gather(panel_rows, "col", axis=1, tiled=True),
             preferred_element_type=jnp.float32,
         )
-        projected = lax.psum(projected.astype(jnp.bfloat16), "row").astype(jnp.float32)
+        projected = jnp.sum(lax.all_gather(projected.astype(jnp.bfloat16), "row"), axis=0).astype(
+            jnp.float32
+        )
         coefficients = jnp.dot(projected, upper_tri[panel_index].T, precision=highest).astype(
             jnp.bfloat16
         )

time: 884 us -> 798 us (0.903)
  waiting for transfers between devices: 340 us -> 243 us
  other arithmetic: 10.9 us -> 20.4 us
    psum x2 -> x0, waiting for transfers between devices: 292 us -> none  [per_device(): lax.psum(projected.astype(jnp.bfloat16), 'row').astype(jnp.float32)]
    all_gather x0 -> x2, waiting for transfers between devices: none -> 199 us  [per_device(): lax.all_gather(projected.astype(jnp.bfloat16), 'row')]
    reduce_sum x0 -> x2, other arithmetic: none -> 9.51 us  [per_device(): jnp.sum(lax.all_gather(projected.astype(jnp.bfloat16), 'row'), axis=0)]
  transfers between devices with their start and end apart: 5 -> 5, of which waited for: 4 -> 4; matrix products, arithmetic and copies ran while one was open for 27% -> 31% of each run, Pallas kernels for 0% -> 0%
where the time goes in v1:
time: 798 us; the launch traced here: 797 us
  blocking collectives  278 us (35%)
  waiting for transfers between devices  243 us (30%)
  local copies, waits for them, and re-layouts  216 us (27%)
  matrix products  25.9 us (3%)
  other arithmetic  20.4 us (3%)
  between operations  13.4 us (2%)
    psum x1, blocking collectives, per_device(): squares = lax.psum(jnp.sum(slice_part * slice_part, axis=0), ('row', 'col'))  278 us
    all_gather x2, waiting for transfers between devices, per_device(): lax.all_gather(projected.astype(jnp.bfloat16), 'row')  199 us
    scatter x1, local copies, waits for them, and re-layouts, per_device(): position = jnp.zeros((order_size,), jnp.int32).at[pole_order].set(jnp.ara...  120 us
    reduce_scatter x1, waiting for transfers between devices, per_device(): lax.psum_scatter(jnp.einsum('ck,rc->kr', mixing, old_block, preferred_ele...  28.4 us
    gather x1, local copies, waits for them, and re-layouts, per_device(): col_live = (1 - deflated[sorted_pos]).astype(jnp.float32)  23 us
    gather x1, local copies, waits for them, and re-layouts, per_device(): col_sq = pole_sq[sorted_pos]  23 us
    gather x1, local copies, waits for them, and re-layouts, per_device(): col_coupling = coupling[sorted_pos]  23 us
  transfers between devices with their start and end apart: 5, of which 4 were waited for; matrix products, arithmetic and copies ran while one was open for 31% of the time, Pallas kernels for 0%

profile of v1, /device:TPU:2, one launch (start us, length us, event | category | flops | bytes accessed | tf_op | source)
XLA Modules:
  0.0 797.3 jit_solution(17121134633861025609)
XLA Ops:
  6.5 0.0 copy-start
  6.5 0.0 copy-start.1
  6.5 0.0 all-gather.9.cloned.1.call-start
  6.5 1.9 fusion.23
  8.4 0.0 all-gather.9.cloned.1.call-update
  8.5 0.0 reduce-scatter.2.cloned.1.call-start
  8.5 0.9 compare_select_fusion
  9.5 120.1 %scatter_custom_fusion = s32[32768]{0:T(1024)S(1)} fusion(s32[32768]{0:T(1024)S(1)} %compare_select_fusion, s32[32768]{0:T(1024)S(1)} %iota.24, s32[]{:T(128)} %constant.25.clone.1), kind=kCustom, calls=%fused_computation.38 | custom fusion | bytes 131076 | tf_op jit(solution)/shard_map/scatter | solution.py:38
  129.6 0.0 copy-done.1
  129.6 23.0 %gather_fusion.2 = s32[4096]{0:T(1024)S(1)} fusion(s32[32768]{0:T(1024)S(1)} %copy-done.1, s32[4096]{0:T(1024)S(1)} %fusion.20), kind=kCustom, calls=%fused_computation.2 | custom fusion | bytes 49152 | tf_op jit(solution)/shard_map/gather | solution.py:43
  152.7 0.0 copy-done
  152.7 0.0 copy-start.4
  152.7 23.0 %gather_fusion.4 = f32[4096]{0:T(1024)S(1)} fusion(f32[32768]{0:T(1024)S(1)} %copy-done, s32[4096]{0:T(1024)S(1)} %fusion.20), kind=kCustom, calls=%fused_computation.4 | custom fusion | bytes 49152 | tf_op jit(solution)/shard_map/gather | solution.py:41
  175.7 0.0 copy-done.4
  175.7 0.0 copy-start.3
  175.7 0.0 copy-start.2
  175.8 6.2 gather_fusion.5
  181.9 6.2 gather_fusion
  188.1 0.0 copy-done.3
  188.1 6.2 gather_fusion.1
  194.3 0.0 copy-done.2
  194.3 0.0 copy-start.5
  194.3 23.0 %gather_fusion.3 = f32[4096]{0:T(1024)S(1)} fusion(f32[32768]{0:T(1024)S(1)} %copy-done.2, s32[4096]{0:T(1024)S(1)} %fusion.20), kind=kCustom, calls=%fused_computation.3 | custom fusion | bytes 49152 | tf_op jit(solution)/shard_map/gather | solution.py:42
  217.3 6.2 gather_fusion.6
  223.5 0.0 copy-done.5
  223.5 6.5 subtract_divide_fusion
  230.0 1.3 multiply_reduce_fusion
  231.3 278.5 %psum.7 = f32[1024]{0:T(1024)S(1)} all-reduce(f32[1024]{0:T(1024)S(1)} %multiply_reduce_fusion), channel_id=1, replica_groups=mesh['side'=2,'row'=32,'col'=4] {'row','col'}, use_global_device_ids=true, to_apply=%region_3.4 | all-reduce | flops 1024 | bytes 8192 | tf_op jit(solution)/shard_map/psum | solution.py:58
  509.8 15.3 %fusion.5 = bf16[1024,1024]{1,0:T(8,128)(2,1)} fusion(bf16[1,1024,4096]{2,1,0:T(8,128)(2,1)} %param.9, s32[1024]{0:T(1024)S(1)} %gather_fusion.1, s32[4096]{0:T(1024)S(1)} %iota_add_fusion, pred[1024]{0:T(1024)(128)(4,1)S(1)} %get-tuple-element.6, f32[1024]{0:T(1024)S(1)} %subtract_multiply_fusion, f32[1024]{0:T(1024)S(1)} %gather_fusion.5, ...), kind=kOutput, calls=%fused_computation.16 | convolution fusion | flops 8620343296 | bytes 10548224 | tf_op jit(solution)/shard_map/ck,rc->kr/dot_general | solution.py:61
  525.2 0.0 reduce-scatter.2.cloned.1.call-update
  525.2 0.0 all-gather.11.cloned.1.call-start
  525.3 0.1 dynamic_slice.11
  525.3 0.0 all-gather.9.cloned.1.call-done
  525.3 28.4 %reduce-scatter.2.cloned.1.call-done = bf16[256,1024]{1,0:T(8,128)(2,1)} async-done(((bf16[1024,1024]{1,0:T(8,128)(2,1)}), bf16[256,1024]{1,0:T(8,128)(2,1)}) %reduce-scatter.2.cloned.1.call-update) | async-done | bytes 524304 | tf_op jit(solution)/shard_map/reduce_scatter | solution.py:60
  553.8 2.6 convolution_convert_fusion.3
  556.4 0.0 all-gather.11.cloned.1.call-update
  556.4 0.0 all-gather.13.cloned.1.call-start
  556.4 0.5 all-gather.13.cloned.1.call-update
  557.0 0.3 all-gather.15.cloned.1.call-start
  557.2 0.2 iota_compare_fusion
  557.5 2.0 bitcast_select_fusion
  559.4 98.5 %all-gather.11.cloned.1.call-done = bf16[8192,512]{1,0:T(8,128)(2,1)} async-done(((bf16[256,512]{1,0:T(8,128)(2,1)}), bf16[8192,512]{1,0:T(8,128)(2,1)}) %all-gather.11.cloned.1.call-update) | async-done | bytes 8388624 | tf_op jit(solution)/shard_map/all_gather | solution.py:83
  657.9 4.8 reduce_sum.34
  662.7 0.7 convolution_convert_fusion.2
  663.4 1.8 convolution_subtract_fusion.1
  665.2 14.9 %all-gather.13.cloned.1.call-done = bf16[1,1,1024,512]{3,2,1,0:T(8,128)(2,1)} async-done(((bf16[1,1,1024,128]{3,2,1,0:T(8,128)(2,1)}), bf16[1,1,1024,512]{3,2,1,0:T(8,128)(2,1)}) %all-gather.13.cloned.1.call-update) | async-done | bytes 1048592 | tf_op jit(solution)/shard_map/all_gather | solution.py:80
  680.2 2.4 convolution_convert_fusion.1
  682.5 0.0 all-gather.15.cloned.1.call-update
  682.6 100.3 %all-gather.15.cloned.1.call-done = bf16[8192,512]{1,0:T(8,128)(2,1)} async-done(((bf16[256,512]{1,0:T(8,128)(2,1)}), bf16[8192,512]{1,0:T(8,128)(2,1)}) %all-gather.15.cloned.1.call-update) | async-done | bytes 8388624 | tf_op jit(solution)/shard_map/all_gather | solution.py:83
  782.9 4.8 reduce_sum.35
  787.6 0.7 convolution_convert_fusion
  788.3 2.5 fusion.9
  (8 shorter events, 0.1 us)
Async XLA Ops:
  6.5 146.1 %copy-start = (f32[32768]{0:T(1024)S(1)}, f32[32768]{0:T(1024)}, u32[]{:S(2)}) copy-start(f32[32768]{0:T(1024)} %param.12) | copy-start | bytes 393220
  6.5 123.1 %copy-start.1 = (s32[32768]{0:T(1024)S(1)}, s32[32768]{0:T(1024)}, u32[]{:S(2)}) copy-start(s32[32768]{0:T(1024)} %param.14) | copy-start | bytes 393220
  6.5 518.8 %all-gather.9.cloned.1.call-start = ((), (), s32[]{:S(2)}) async-start(), calls=%async_computation.2 | async-start | bytes 1310720 | tf_op jit(solution)/shard_map/all_gather | solution.py:80
  8.5 545.3 %reduce-scatter.2.cloned.1.call-start = ((), (), s32[]{:S(2)}) async-start(), calls=%async_computation.1 | async-start | bytes 2621440 | tf_op jit(solution)/shard_map/reduce_scatter | solution.py:60
  152.7 23.1 %copy-start.4 = (s32[1024]{0:T(1024)S(1)}, s32[1024]{0:T(1024)}, u32[]{:S(2)}) copy-start(s32[1024]{0:T(1024)} %param.16) | copy-start | bytes 12292
  175.7 12.4 %copy-start.3 = (s32[32768]{0:T(1024)S(1)}, s32[32768]{0:T(1024)}, u32[]{:S(2)}) copy-start(s32[32768]{0:T(1024)} %param.15) | copy-start | bytes 393220
  175.7 18.5 %copy-start.2 = (f32[32768]{0:T(1024)S(1)}, f32[32768]{0:T(1024)}, u32[]{:S(2)}) copy-start(f32[32768]{0:T(1024)} %param.13) | copy-start | bytes 393220
  194.3 29.2 %copy-start.5 = (f32[1024]{0:T(1024)S(1)}, f32[1024]{0:T(1024)}, u32[]{:S(2)}) copy-start(f32[1024]{0:T(1024)} %param.17) | copy-start | bytes 12292
  525.2 132.7 %all-gather.11.cloned.1.call-start = ((), (), s32[]{:S(2)}) async-start(), calls=%async_computation.3 | async-start | bytes 8650752 | tf_op jit(solution)/shard_map/all_gather | solution.py:83
  556.4 123.8 %all-gather.13.cloned.1.call-start = ((), (), s32[]{:S(2)}) async-start(), calls=%async_computation.4 | async-start | bytes 1310720 | tf_op jit(solution)/shard_map/all_gather | solution.py:80
  557.0 225.9 %all-gather.15.cloned.1.call-start = ((), (), s32[]{:S(2)}) async-start(), calls=%async_computation.5 | async-start | bytes 8650752 | tf_op jit(solution)/shard_map/all_gather | solution.py:83
Sparse Core Ops, SparseCore 0:
  9.2 26.2 all-gather.8
  525.3 28.4 reduce-scatter.1
  556.7 101.1 all-gather.10
  659.7 20.3 all-gather.12
  682.9 99.8 all-gather.14
